TPU v7x, 512 devices: a whole 4x4x16 slice. The times are simulated.
512 devices in a mesh: tok: 16 (over z), head: 8 (over x, core), vid: 4 (over y).
Axes of the slice: x: 4, y: 4, z: 16, core: 2. Of those that a mesh axis runs over, the one named last changes fastest.
Arguments:
- queries: bfloat16 [4, 3, 2048, 8, 256], P('vid', None, 'tok', 'head'), may hold values from -6 to 6
- keys: bfloat16 [4, 3, 2048, 8, 256], P('vid', None, 'tok', 'head'), may hold values from -6 to 6
- values: bfloat16 [4, 3, 2048, 8, 256], P('vid', None, 'tok', 'head'), may hold values from -6 to 6
- out_grad: bfloat16 [4, 3, 2048, 8, 256], P('vid', None, 'tok', 'head'), may hold values from -6 to 6
- fast_init: bfloat16 [8, 3, 256, 256], P('head'), may hold values from -0.375 to 0.375
- updates: bfloat16 [4, 2, 8, 3, 256, 256], P('vid', None, 'head'), may hold values from -4 to 4
Outputs:
- query_grad: bfloat16 [4, 3, 2048, 8, 256], P('vid', None, 'tok', 'head')
- key_grad: bfloat16 [4, 3, 2048, 8, 256], P('vid', None, 'tok', 'head')
- value_grad: bfloat16 [4, 3, 2048, 8, 256], P('vid', None, 'tok', 'head')
- init_grad: float32 [8, 3, 256, 256], P('head')
All inputs are finite; a program needn't handle non-finite values.
Results may differ from a plain program's by a relative error of at most 0.0014.
Values sent between devices are 32-bit elements; how exact they have to be, the bound alone decides.
A program may use at most 64 MiB of HBM per device.

v0:
```python
import jax
import jax.numpy as jnp
from jax import lax
from jax.sharding import PartitionSpec as P

EPS = 1e-06
HIGH = lax.Precision.HIGHEST


def matmul(left, right):
    return jnp.dot(left, right, precision=HIGH, preferred_element_type=jnp.float32)


def swiglu(rows, weights):
    gate = matmul(rows, weights[0])
    upper = matmul(rows, weights[1])
    return matmul(jax.nn.silu(gate) * upper, weights[2])


def update(weights, key_rows, value_rows, scale):
    gate = matmul(key_rows, weights[0])
    upper = matmul(key_rows, weights[1])
    active = jax.nn.silu(gate)
    sigma = jax.nn.sigmoid(gate)
    down_step = matmul((active * upper).T, value_rows)
    back = matmul(value_rows, weights[2].T)
    gate_step = matmul(key_rows.T, back * upper * sigma * (1.0 + gate * (1.0 - sigma)))
    up_step = matmul(key_rows.T, back * active)
    return jnp.stack([gate_step, up_step, down_step]) * scale


def colnorm(weights, raised):
    old = jnp.sqrt(jnp.sum(weights * weights, axis=-2) + EPS)
    new = jnp.sqrt(jnp.sum(raised * raised, axis=-2) + EPS)
    return raised * (old / new)[..., None, :]


def group_back(weights, query, key_rows, value_rows, cot, upper_adj, scale):

    def group_local(wt, qq, kk, vv, cc, adj):

        def forward(first, second, third, fourth):
            return (swiglu(second, first), update(first, third, fourth, scale))

        _, back = jax.vjp(forward, wt, qq, kk, vv)
        return back((cc, adj))

    inner = jax.vmap(group_local, in_axes=(0, 1, 1, 1, 1, 0), out_axes=(0, 1, 1, 1))
    return jax.vmap(inner)(weights, query, key_rows, value_rows, cot, upper_adj)


def apply_back(weights, query, cot):

    def apply_local(wt, qq, cc):
        _, back = jax.vjp(swiglu, qq, wt)
        return back(cc)

    inner = jax.vmap(apply_local, in_axes=(0, 1, 1), out_axes=(1, 0))
    return jax.vmap(inner)(weights, query, cot)


def local_terms(index, groups, weights, queries, keys, values, out_grad, upper_adj, scale):
    query = queries[:, index].astype(jnp.float32)
    cot = out_grad[:, index].astype(jnp.float32)
    if index + 1 < groups:
        key_rows = keys[:, index].astype(jnp.float32)
        value_rows = values[:, index].astype(jnp.float32)
        wpart, dq, dk, dv = group_back(
            weights[index], query, key_rows, value_rows, cot, upper_adj, scale
        )
    else:
        dq, wpart = apply_back(weights[index], query, cot)
        dk = jnp.zeros(query.shape, jnp.float32)
        dv = jnp.zeros(query.shape, jnp.float32)
    return (wpart, dq, dk, dv)


def on_device(queries, keys, values, out_grad, fast_init, updates):
    tok_count = lax.axis_size("tok")
    scale = float(queries.shape[2] * tok_count) ** (-0.5)
    vids = queries.shape[0]
    groups = queries.shape[1]
    init = fast_init.astype(jnp.float32)
    steps = updates.astype(jnp.float32)
    weights = [init[None]]
    for index in range(groups - 1):
        weights.append(colnorm(weights[index], weights[index] + steps[:, index]))
    zero_adj = jnp.zeros(weights[0].shape, jnp.float32)
    grads_q, grads_k, grads_v = ([], [], [])
    adjoint = zero_adj
    for index in reversed(range(groups)):
        current = weights[index]
        if index + 1 < groups:
            _, norm_back = jax.vjp(colnorm, current, current + steps[:, index])
            direct, upper_adj = norm_back(adjoint)
        else:
            direct, upper_adj = (zero_adj, zero_adj)
        wpart, dq, dk, dv = local_terms(
            index, groups, weights, queries, keys, values, out_grad, upper_adj, scale
        )
        adjoint = direct + upper_adj + lax.psum(wpart, "tok")
        grads_q.append(dq)
        grads_k.append(dk)
        grads_v.append(dv)
    init_grad = lax.psum(jnp.sum(adjoint, axis=0), "vid")

    def stacked(items):
        return jnp.stack(items[::-1], axis=1).astype(jnp.bfloat16)

    return (stacked(grads_q), stacked(grads_k), stacked(grads_v), init_grad)


def solution(mesh):
    return jax.shard_map(
        on_device,
        mesh=mesh,
        in_specs=(
            P("vid", None, "tok", "head", None),
            P("vid", None, "tok", "head", None),
            P("vid", None, "tok", "head", None),
            P("vid", None, "tok", "head", None),
            P("head", None, None, None),
            P("vid", None, "head", None, None, None),
        ),
        out_specs=(
            P("vid", None, "tok", "head", None),
            P("vid", None, "tok", "head", None),
            P("vid", None, "tok", "head", None),
            P("head", None, None, None),
        ),
        check_vma=False,
    )
```

profile of v0, /device:TPU:6, one launch (start us, length us, event | category | flops | bytes accessed | tf_op | source)
XLA Modules:
  0.0 508.5 jit_solution(4007719239524762023)
XLA Ops:
  7.2 1.3 convert_element_type.44
  9.6 0.7 copy-done.14
  12.2 0.9 pad_add_fusion.2
  13.2 1.0 fusion.96
  14.3 1.1 fusion.94
  15.4 1.0 fusion.98
  16.7 1.0 convolution_bitcast_fusion.1
  18.7 0.4 fusion.37
  19.1 1.0 convolution_bitcast_fusion.6
  20.1 1.0 convolution_bitcast_fusion.8
  21.1 0.4 fusion.31
  21.6 0.8 fusion.95
  22.4 0.8 fusion.93
  23.2 1.0 convolution_bitcast_fusion.2
  24.3 0.9 fusion.18
  25.2 1.0 fusion.17
  26.2 1.0 fusion.16
  27.2 1.1 convolution_bitcast_fusion.7
  28.3 0.9 fusion.35
  29.2 0.9 fusion.36
  30.1 0.9 fusion.34
  31.0 125.3 %all-reduce.20.cloned.1.call-done = f32[1,1,3,256,256]{4,3,2,1,0:T(8,128)} async-done(((f32[1,1,3,256,256]{4,3,2,1,0:T(8,128)}), f32[1,1,3,256,256]{4,3,2,1,0:T(8,128)}) %all-reduce.20.cloned.1.call-update) | async-done | bytes 786448 | tf_op jit(solution)/shard_map/psum | solution.py:101
  156.4 1.3 multiply_reduce_fusion.1
  157.7 1.3 multiply_multiply_fusion.1
  161.5 1.0 pad_add_fusion.1
  162.8 1.7 pad_maximum_fusion
  164.5 0.6 pad.65.clone
  165.1 2.1 convolution_bitcast_fusion
  167.2 1.7 fusion.97
  168.8 1.0 convolution_bitcast_fusion.18
  169.9 1.5 convolution_bitcast_fusion.15
  171.4 1.2 fusion.21
  172.7 125.2 %all-reduce.22.cloned.1.call-done = f32[1,1,3,256,256]{4,3,2,1,0:T(8,128)} async-done(((f32[1,1,3,256,256]{4,3,2,1,0:T(8,128)}), f32[1,1,3,256,256]{4,3,2,1,0:T(8,128)}) %all-reduce.22.cloned.1.call-update) | async-done | bytes 786448 | tf_op jit(solution)/shard_map/psum | solution.py:101
  297.9 1.8 multiply_reduce_fusion
  299.7 0.6 multiply_multiply_fusion
  300.4 1.4 broadcast_multiply_fusion
  304.2 1.0 pad_add_fusion
  305.6 1.5 fusion.32
  307.1 1.5 fusion
  309.0 0.6 convolution_bitcast_fusion.17
  309.9 130.6 %all-reduce.24.cloned.1.call-done = f32[1,1,3,256,256]{4,3,2,1,0:T(8,128)} async-done(((f32[1,1,3,256,256]{4,3,2,1,0:T(8,128)}), f32[1,1,3,256,256]{4,3,2,1,0:T(8,128)}) %all-reduce.24.cloned.1.call-update) | async-done | bytes 786448 | tf_op jit(solution)/shard_map/psum | solution.py:101
  440.5 2.2 fusion.27
  443.1 0.4 fusion.33
  443.6 0.4 fusion.1
  444.5 0.8 copy.42
  445.3 0.8 copy.41
  446.1 53.8 %all-reduce.26.cloned.1.call-done = f32[1,3,256,256]{3,2,1,0:T(8,128)} async-done(((f32[1,3,256,256]{3,2,1,0:T(8,128)}), f32[1,3,256,256]{3,2,1,0:T(8,128)}) %all-reduce.26.cloned.1.call-update) | async-done | bytes 786448 | tf_op jit(solution)/shard_map/psum | solution.py:105
  499.9 2.1 copy.78
  (181 shorter events, 10.7 us)
Async XLA Ops:
  7.2 149.2 %all-reduce.20.cloned.1.call-start = ((), (), s32[]{:S(2)}) async-start(), calls=%async_computation | async-start | bytes 1572864 | tf_op jit(solution)/shard_map/psum | solution.py:101
  9.3 2.1 copy-start.66
  10.3 1.9 copy-start.3
  10.5 1.6 copy-start.54
  13.1 284.7 %all-reduce.22.cloned.1.call-start = ((), (), s32[]{:S(2)}) async-start(), calls=%async_computation.1 | async-start | bytes 1572864 | tf_op jit(solution)/shard_map/psum | solution.py:101
  13.2 3.6 copy-start.15
  13.2 4.8 copy-start.53
  14.3 10.0 %copy-start.60 = (f32[128,256]{1,0:T(8,128)}, f32[128,256]{1,0:T(8,128)S(1)}, u32[]{:S(2)}) copy-start(f32[128,256]{1,0:T(8,128)S(1)} %fusion.96) | copy-start | bytes 393220
  15.3 8.9 %copy-start.61 = (f32[128,256]{1,0:T(8,128)}, f32[128,256]{1,0:T(8,128)S(1)}, u32[]{:S(2)}) copy-start(f32[128,256]{1,0:T(8,128)S(1)} %fusion.94) | copy-start | bytes 393220
  16.4 7.9 %copy-start.62 = (f32[128,256]{1,0:T(8,128)}, f32[128,256]{1,0:T(8,128)S(1)}, u32[]{:S(2)}) copy-start(f32[128,256]{1,0:T(8,128)S(1)} %fusion.98) | copy-start | bytes 393220
  18.0 3.1 copy-start.4
  18.0 3.1 copy-start.55
  18.1 3.1 copy-start.59
  18.4 3.2 copy-start.11
  18.6 3.7 copy-start.16
  21.6 4.7 copy-start.57
  156.4 2.7 copy-start.1
  157.7 1.8 copy-start.12
  159.2 1.9 copy-start.5
  162.5 278.0 %all-reduce.24.cloned.1.call-start = ((), (), s32[]{:S(2)}) async-start(), calls=%async_computation.2 | async-start | bytes 1572864 | tf_op jit(solution)/shard_map/psum | solution.py:101
  162.7 6.1 %copy-start.43 = (f32[128,256]{1,0:T(8,128)S(1)}, f32[128,256]{1,0:T(8,128)}, u32[]{:S(2)}) copy-start(f32[128,256]{1,0:T(8,128)} %copy-done.42) | copy-start | bytes 393220
  162.7 7.1 %copy-start.20 = (f32[256,128]{0,1:T(8,128)S(1)}, f32[256,128]{0,1:T(8,128)}, u32[]{:S(2)}) copy-start(f32[256,128]{0,1:T(8,128)} %fusion.35) | copy-start | bytes 393220
  162.8 7.1 %copy-start.22 = (f32[256,128]{0,1:T(8,128)S(1)}, f32[256,128]{0,1:T(8,128)}, u32[]{:S(2)}) copy-start(f32[256,128]{0,1:T(8,128)} %fusion.36) | copy-start | bytes 393220
  162.8 8.6 %copy-start.41 = (f32[128,256]{1,0:T(8,128)S(1)}, f32[128,256]{1,0:T(8,128)}, u32[]{:S(2)}) copy-start(f32[128,256]{1,0:T(8,128)} %copy-done.40) | copy-start | bytes 393220
  297.9 1.9 copy-start.64
  297.9 2.5 copy-start.2
  297.9 2.5 copy-start.10
  297.9 2.5 copy-start.67
  300.3 1.7 copy-start.18
  300.4 2.0 copy-start.28
  300.4 2.0 copy-start.31
  300.4 2.0 copy-start.33
  301.8 2.0 copy-start.7
  302.4 1.7 copy-start.45
  302.4 1.7 copy-start.46
  302.4 1.7 copy-start.47
  305.2 3.8 copy-start.8
  305.2 135.3 %copy-start.9 = (f32[1,1,3,256,256]{4,3,2,1,0:T(8,128)S(1)}, f32[1,1,3,256,256]{4,3,2,1,0:T(8,128)}, u32[]{:S(2)}) copy-start(f32[1,1,3,256,256]{4,3,2,1,0:T(8,128)} %get-tuple-element.11) | copy-start | bytes 2359300
  305.2 135.3 %copy-start.68 = (f32[3,256]{1,0:T(4,128)S(1)}, f32[3,256]{1,0:T(4,128)}, u32[]{:S(2)}) copy-start(f32[3,256]{1,0:T(4,128)} %get-tuple-element.21) | copy-start | bytes 9220
  305.2 194.7 %all-reduce.26.cloned.1.call-start = ((), (), s32[]{:S(2)}) async-start(), calls=%async_computation.3 | async-start | bytes 1572864 | tf_op jit(solution)/shard_map/psum | solution.py:105
  305.5 3.0 copy-start.37
  305.5 3.0 copy-start.44
  305.5 3.4 copy-start.29
  305.5 3.4 copy-start.34
  305.5 4.0 copy-start.27
  440.5 2.2 copy-start.25
  440.5 2.5 copy-start.30
  440.5 2.5 copy-start.32
  (26 other events, 29.2 us)
Sparse Core Ops, SparseCore 0:
  13.2 143.0 all-reduce.19
  162.6 135.1 all-reduce.21
  305.3 135.1 all-reduce.23
  443.3 56.5 all-reduce.25
where the time goes:
time: 509 us
  waiting for transfers between devices  435 us (85%)
  matrix products  36.2 us (7%)
  other arithmetic  15.4 us (3%)
  between operations  14.8 us (3%)
  local copies, waits for them, and re-layouts  6.78 us (1%)
    psum x3, waiting for transfers between devices, on_device(): adjoint = direct + upper_adj + lax.psum(wpart, 'tok')  381 us
    psum x1, waiting for transfers between devices, on_device(): init_grad = lax.psum(jnp.sum(adjoint, axis=0), 'vid')  53.8 us
    dot_general x54, matrix products, matmul(): jnp.dot(left, right, precision=HIGH, preferred_element_type=jnp.float32)  36.2 us
  transfers between devices with their start and end apart: 4, of which 4 were waited for; matrix products, arithmetic and copies ran while one was open for 7% of the time, Pallas kernels for 0%

commit v1 on v0

v1 whole, which is shorter than its diff:
```python
import functools

import jax
import jax.numpy as jnp
from jax import lax
from jax.experimental import pallas as pl
from jax.experimental.pallas import tpu as pltpu
from jax.sharding import PartitionSpec as P

EPS = 1e-06
F32 = jnp.float32
BF16 = jnp.bfloat16
ROWS_PER_PIECE = 16


def nn(a, b):
    return lax.dot_general(a, b, (((1,), (0,)), ((), ())), preferred_element_type=F32)


def nt(a, b):
    return lax.dot_general(a, b, (((1,), (1,)), ((), ())), preferred_element_type=F32)


def split(x):
    hi = x.astype(BF16)
    return hi, (x - hi.astype(F32)).astype(BF16)


def kernel(
    n, nv, scale,
    q_h, k_h, v_h, o_h, init_h, upd_h,
    dq_r, dk_r, dv_r, ig_r,
    qv, kv, vv, ov, iv, uv,
    wb, ub, ut, mb, sv, pu, act, tt, rb, vb,
    in_sem, rs_ss, rs_rs, ag_ss, ag_rs, v_ss, v_rs,
):
    hd = iv.shape[1]
    sr = hd // n
    half = n // 2
    rp = min(ROWS_PER_PIECE, sr)
    pieces = [(m, r) for m in range(3) for r in range(0, sr, rp)]

    me = lax.axis_index("tok")
    core = lax.rem(lax.axis_index("head"), 2)
    vid = lax.axis_index("vid")
    flip = lambda i: lax.rem(i * (1 - core) + (n - i) * core, n)
    p = flip(me)
    nxt = flip(lax.rem(p + 1, n))
    prv = flip(lax.rem(p + n - 1, n))

    barrier = pltpu.get_barrier_semaphore()
    for z in (nxt, prv):
        pl.semaphore_signal(barrier, inc=1, device_id={"tok": z}, device_id_type=pl.DeviceIdType.MESH)
    for d in range(1, nv):
        pl.semaphore_signal(
            barrier, inc=1, device_id={"vid": lax.rem(vid + d, nv)}, device_id_type=pl.DeviceIdType.MESH
        )

    loads = {}

    def load(name, src, dst, i):
        loads[name] = pltpu.make_async_copy(src, dst, in_sem.at[i])
        loads[name].start()

    load("init", init_h, iv, 0)
    load("upd0", upd_h.at[0], uv.at[0], 1)
    load("upd1", upd_h.at[1], uv.at[1], 2)
    load("q2", q_h.at[2], qv.at[2], 3)
    load("o2", o_h.at[2], ov.at[2], 4)
    load("k1", k_h.at[1], kv.at[1], 5)
    load("v1", v_h.at[1], vv.at[1], 6)
    load("q1", q_h.at[1], qv.at[1], 7)
    load("o1", o_h.at[1], ov.at[1], 8)
    load("k0", k_h.at[0], kv.at[0], 9)
    load("v0", v_h.at[0], vv.at[0], 10)
    load("q0", q_h.at[0], qv.at[0], 11)
    load("o0", o_h.at[0], ov.at[0], 12)

    def rows(shard, r=0, size=None):
        return pl.ds(pl.multiple_of(lax.rem(shard + 2 * n, n) * sr + r, 8), size or rp)

    def weights():
        for name in ("init", "upd0", "upd1"):
            loads[name].wait()
        for m in range(3):
            w = iv[m].astype(F32)
            for c in range(3):
                hi, lo = split(w)
                wb[c, m, 0] = hi
                wb[c, m, 1] = lo
                if c < 2:
                    up = w + uv[c, m].astype(F32)
                    old = jnp.sqrt(jnp.sum(w * w, axis=0, keepdims=True) + EPS)
                    new = jnp.sqrt(jnp.sum(up * up, axis=0, keepdims=True) + EPS)
                    w = up * (old / new)

    def xw(x, c, m):
        return nn(x, wb[c, m, 0]) + nn(x, wb[c, m, 1])

    def xwt(x, c, m):
        return nt(x, wb[c, m, 0]) + nt(x, wb[c, m, 1])

    def ywt(y, c, m):
        hi, lo = split(y)
        return nt(hi, wb[c, m, 0]) + nt(hi, wb[c, m, 1]) + nt(lo, wb[c, m, 0])

    def yw(y, c, m):
        hi, lo = split(y)
        return nn(hi, wb[c, m, 0]) + nn(hi, wb[c, m, 1]) + nn(lo, wb[c, m, 0])

    def left2(y, x):
        hi, lo = split(y)
        return nn(hi, x) + nn(lo, x)

    def right2(x, y):
        hi, lo = split(y)
        return nn(x, hi) + nn(x, lo)

    def t16(x):
        return x.astype(F32).T.astype(BF16)

    def query_a(c):
        loads[f"q{c}"].wait()
        loads[f"o{c}"].wait()
        g = xw(qv[c], c, 0)
        u = xw(qv[c], c, 1)
        dh = xwt(ov[c], c, 2)
        s = jax.nn.sigmoid(g)
        a = g * s
        act[0] = dh * u * (s * (1.0 + g * (1.0 - s)))
        act[1] = dh * a
        act[2] = a * u

    def query_b(c):
        if c > 0:
            mb[c, 0] = left2(act[0].T, qv[c])
            mb[c, 1] = left2(act[1].T, qv[c])
            mb[c, 2] = right2(t16(ov[c]), act[2])
        else:
            qt = t16(qv[c])
            mb[c, 0] = right2(qt, act[0])
            mb[c, 1] = right2(qt, act[1])
            mb[c, 2] = left2(act[2].T, ov[c])

    def query_c(c):
        dq_r[c] = (ywt(act[0], c, 0) + ywt(act[1], c, 1)).astype(BF16)

    def update_a(c):
        loads[f"k{c}"].wait()
        loads[f"v{c}"].wait()
        g = xw(kv[c], c, 0)
        u = xw(kv[c], c, 1)
        b = xwt(vv[c], c, 2)
        s = jax.nn.sigmoid(g)
        a = g * s * scale
        d1 = (s * (1.0 + g * (1.0 - s))) * scale
        d2 = (s * (1.0 - s) * (2.0 + g * (1.0 - 2.0 * s))) * scale
        act[3] = b * u * d2
        act[4] = b * d1
        act[5] = u * d1
        act[6] = a
        act[7] = b * u * d1
        act[8] = b * a
        act[9] = a * u

    def update_t(c):
        if c > 0:
            tt[...] = t16(vv[c])
        else:
            tt[...] = t16(kv[c])

    def kut(c, m):
        return nt(kv[c], ub[m, 0]) + nt(kv[c], ub[m, 1])

    def update_b(c):
        for m in range(3):
            hi, lo = split(ut[c, m])
            ub[m, 0] = hi
            ub[m, 1] = lo
        d_gate = kut(c, 0)
        d_up = kut(c, 1)
        dh = nn(vv[c], ub[2, 0]) + nn(vv[c], ub[2, 1])
        gb = d_gate * act[3] + d_up * act[4] + dh * act[5]
        u_b = d_gate * act[4] + dh * act[6]
        bb = d_gate * act[5] + d_up * act[6]
        act[0] = gb
        act[1] = u_b
        act[2] = bb
        if c > 0:
            mb[c, 0] += left2(gb.T, kv[c])
            mb[c, 1] += left2(u_b.T, kv[c])
            mb[c, 2] += right2(tt[...], bb)
        else:
            mb[c, 0] += right2(tt[...], gb)
            mb[c, 1] += right2(tt[...], u_b)
            mb[c, 2] += left2(bb.T, vv[c])

    def dot3(y, m, transposed):
        hi, lo = split(y)
        f = nt if transposed else nn
        return f(hi, ub[m, 0]) + f(hi, ub[m, 1]) + f(lo, ub[m, 0])

    def grads_a(c):
        dk_r[c] = (
            dot3(act[7], 0, False) + dot3(act[8], 1, False) + ywt(act[0], c, 0) + ywt(act[1], c, 1)
        ).astype(BF16)

    def grads_b(c):
        dv_r[c] = (dot3(act[9], 2, True) + yw(act[2], c, 2)).astype(BF16)

    def shard_rows():
        at = lax.broadcasted_iota(jnp.int32, (sr, hd), 1) - lax.broadcasted_iota(jnp.int32, (sr, hd), 0)
        pick = jnp.where(at == p * sr, 1.0, 0.0).astype(BF16)
        for m in range(3):
            w = nt(pick, iv[m])
            for c in range(2):
                up = w + nt(pick, uv[c, m])
                old = jnp.sqrt(jnp.sum(w * w, axis=1, keepdims=True) + EPS)
                new = jnp.sqrt(jnp.sum(up * up, axis=1, keepdims=True) + EPS)
                ratio = old / new
                sv[c, 0, m] = up
                sv[c, 1, m] = jnp.broadcast_to(ratio, up.shape)
                sv[c, 2, m] = up * (ratio / (new * new))
                sv[c, 3, m] = w / (old * new)
                w = up * ratio

    def place():
        at = lax.broadcasted_iota(jnp.int32, (sr, hd), 1) - lax.broadcasted_iota(jnp.int32, (sr, hd), 0)
        pick = jnp.where(at == p * sr, 1.0, 0.0)
        for m in range(3):
            mb[0, m] += lax.dot_general(
                pu[m], pick, (((0,), (0,)), ((), ())),
                precision=lax.Precision.HIGHEST, preferred_element_type=F32,
            )

    def copy_to(axis, index, src, dst, ss, rs):
        return pltpu.make_async_remote_copy(
            src_ref=src, dst_ref=dst, send_sem=ss, recv_sem=rs,
            device_id={axis: index}, device_id_type=pl.DeviceIdType.MESH,
        )

    def work(queue):
        if queue:
            queue.pop(0)()

    def reduce_scatter(c, queue, finish):
        sent = []
        for s in range(half):
            for i, (m, r) in enumerate(pieces):
                for d, (to, count) in enumerate(((prv, half), (nxt, n - 1 - half))):
                    if s >= count:
                        continue
                    shard = p - half + s if d == 0 else p + (n - 1 - half) - s
                    own = mb.at[c, m, rows(shard, r)]
                    src = own
                    if s:
                        src = rb.at[c, d, s - 1, m, pl.ds(r, rp)]
                        copy_to("tok", to, src, src, rs_ss.at[d, s - 1, i], rs_rs.at[d, s - 1, i]).wait_recv()
                        src[...] += own[...]
                    cp = copy_to("tok", to, src, rb.at[c, d, s, m, pl.ds(r, rp)], rs_ss.at[d, s, i], rs_rs.at[d, s, i])
                    cp.start()
                    sent.append(cp)
            work(queue)
        for i, (m, r) in enumerate(pieces):
            total = mb[c, m, rows(p, r)]
            for d, count in ((0, half), (1, n - 1 - half)):
                if count:
                    src = rb.at[c, d, count - 1, m, pl.ds(r, rp)]
                    copy_to("tok", nxt, src, src, rs_ss.at[d, count - 1, i], rs_rs.at[d, count - 1, i]).wait_recv()
                    total = total + src[...]
            finish(i, m, r, total)
        for cp in sent:
            cp.wait_send()

    def gather_send(buf, s, i, m, r, d, sent):
        to = nxt if d == 0 else prv
        shard = p - s if d == 0 else p + s
        at = buf.at[m, rows(shard, r)]
        cp = copy_to("tok", to, at, at, ag_ss.at[d, s, i], ag_rs.at[d, s, i])
        cp.start()
        sent.append(cp)

    def gather_rest(buf, queue, sent):
        for s in range(1, half + 1):
            for i, (m, r) in enumerate(pieces):
                for d, count in ((0, half), (1, n - 1 - half)):
                    if s > count:
                        continue
                    shard = p - s if d == 0 else p + s
                    at = buf.at[m, rows(shard, r)]
                    copy_to("tok", nxt, at, at, ag_ss.at[d, s - 1, i], ag_rs.at[d, s - 1, i]).wait_recv()
                    if s < count:
                        gather_send(buf, s, i, m, r, d, sent)
            if s < half:
                work(queue)
        for cp in sent:
            cp.wait_send()

    def norm_back(c, first):
        sent = []

        def finish(i, m, r, total):
            at = pl.ds(r, rp)
            if not first:
                total = total + pu[m, at]
            inner = jnp.sum(total * sv[c, 0, m, at], axis=1, keepdims=True)
            step = total * sv[c, 1, m, at] - inner * sv[c, 2, m, at]
            ut[c, m, rows(p, r)] = step
            gather_send(ut.at[c], 0, i, m, r, 0, sent)
            if n - 1 - half:
                gather_send(ut.at[c], 0, i, m, r, 1, sent)
            pu[m, at] = step + inner * sv[c, 3, m, at]

        return finish, sent

    weights()
    query_a(2)
    query_b(2)
    pl.semaphore_wait(barrier, 2 + nv - 1)

    def zeros():
        dk_r[2] = jnp.zeros(dk_r.shape[1:], BF16)
        dv_r[2] = jnp.zeros(dv_r.shape[1:], BF16)

    finish, sent = norm_back(1, True)
    queue = [
        lambda: (shard_rows(), zeros()), lambda: query_c(2), lambda: update_a(1), lambda: update_t(1),
        lambda: query_a(1), lambda: query_b(1), lambda: query_c(1),
    ]
    reduce_scatter(2, queue, finish)
    gather_rest(ut.at[1], queue, sent)
    while queue:
        work(queue)
    update_b(1)

    finish, sent = norm_back(0, False)
    queue = [
        lambda: grads_a(1), lambda: grads_b(1), lambda: update_a(0), lambda: update_t(0),
        lambda: query_a(0), lambda: query_b(0), lambda: query_c(0),
    ]
    reduce_scatter(1, queue, finish)
    queue.append(place)
    gather_rest(ut.at[0], queue, sent)
    while queue:
        work(queue)
    update_b(0)

    vsent = []
    queue = [lambda: grads_a(0), lambda: grads_b(0)]

    def to_videos(i, m, r, total):
        at = vb.at[vid, m, pl.ds(r, rp)]
        at[...] = total
        for d in range(1, nv):
            cp = copy_to("vid", lax.rem(vid + d, nv), at, at, v_ss.at[d, i], v_rs.at[d, i])
            cp.start()
            vsent.append(cp)

    reduce_scatter(0, queue, to_videos)
    sent = []
    for i, (m, r) in enumerate(pieces):
        for d in range(1, nv):
            at = vb.at[lax.rem(vid + nv - d, nv), m, pl.ds(r, rp)]
            copy_to("vid", vid, at, at, v_ss.at[d, i], v_rs.at[d, i]).wait_recv()
        total = vb[0, m, pl.ds(r, rp)]
        for w in range(1, nv):
            total = total + vb[w, m, pl.ds(r, rp)]
        ig_r[m, rows(p, r)] = total
        gather_send(ig_r, 0, i, m, r, 0, sent)
        if n - 1 - half:
            gather_send(ig_r, 0, i, m, r, 1, sent)
    for cp in vsent:
        cp.wait_send()
    gather_rest(ig_r, queue, sent)


def on_device(n, nv, queries, keys, values, out_grad, fast_init, updates):
    _, groups, tokens, _, hd = queries.shape
    scale = float(tokens * n) ** (-0.5)
    half = n // 2
    sr = hd // n
    pc = 3 * (sr // min(ROWS_PER_PIECE, sr))
    flat = lambda x: x.reshape(groups, tokens, hd)
    anyspec = pl.BlockSpec(memory_space=pl.ANY)
    vspec = pl.BlockSpec(memory_space=pltpu.VMEM)
    dma = pltpu.SemaphoreType.DMA
    tok_shape = jax.ShapeDtypeStruct((groups, tokens, hd), BF16)
    dq, dk, dv, ig = pl.pallas_call(
        functools.partial(kernel, n, nv, scale),
        out_shape=(tok_shape, tok_shape, tok_shape, jax.ShapeDtypeStruct((3, hd, hd), F32)),
        in_specs=[anyspec] * 6,
        out_specs=[vspec] * 4,
        scratch_shapes=[
            pltpu.VMEM((groups, tokens, hd), BF16),
            pltpu.VMEM((groups, tokens, hd), BF16),
            pltpu.VMEM((groups, tokens, hd), BF16),
            pltpu.VMEM((groups, tokens, hd), BF16),
            pltpu.VMEM((3, hd, hd), BF16),
            pltpu.VMEM((2, 3, hd, hd), BF16),
            pltpu.VMEM((3, 3, 2, hd, hd), BF16),
            pltpu.VMEM((3, 2, hd, hd), BF16),
            pltpu.VMEM((2, 3, hd, hd), F32),
            pltpu.VMEM((3, 3, hd, hd), F32),
            pltpu.VMEM((2, 4, 3, sr, hd), F32),
            pltpu.VMEM((3, sr, hd), F32),
            pltpu.VMEM((10, tokens, hd), F32),
            pltpu.VMEM((hd, tokens), BF16),
            pltpu.VMEM((3, 2, half, 3, sr, hd), F32),
            pltpu.VMEM((nv, 3, sr, hd), F32),
            dma((13,)),
            dma((2, half, pc)), dma((2, half, pc)),
            dma((2, half, pc)), dma((2, half, pc)),
            dma((nv, pc)), dma((nv, pc)),
        ],
        compiler_params=pltpu.CompilerParams(
            collective_id=0, has_side_effects=True, vmem_limit_bytes=48 * 1024 * 1024
        ),
    )(
        flat(queries), flat(keys), flat(values), flat(out_grad),
        fast_init.reshape(3, hd, hd), updates.reshape(groups - 1, 3, hd, hd),
    )
    shaped = lambda x: x.reshape(queries.shape)
    return shaped(dq), shaped(dk), shaped(dv), ig.reshape(fast_init.shape)


def solution(mesh):
    return jax.shard_map(
        functools.partial(on_device, mesh.shape["tok"], mesh.shape["vid"]),
        mesh=mesh,
        in_specs=(
            P("vid", None, "tok", "head", None),
            P("vid", None, "tok", "head", None),
            P("vid", None, "tok", "head", None),
            P("vid", None, "tok", "head", None),
            P("head", None, None, None),
            P("vid", None, "head", None, None, None),
        ),
        out_specs=(
            P("vid", None, "tok", "head", None),
            P("vid", None, "tok", "head", None),
            P("vid", None, "tok", "head", None),
            P("head", None, None, None),
        ),
        check_vma=False,
    )
```

time: 509 us -> 179 us (0.35)
  waiting for transfers between devices: 435 us -> 0 us
  Pallas kernels: 0 us -> 170 us
  matrix products: 36.2 us -> 0 us
  other arithmetic: 15.4 us -> 0 us
  between operations: 14.8 us -> 0.66 us
    psum x4 -> x0, waiting for transfers between devices: 435 us -> none  [the longest x3 381 us: on_device(): adjoint = direct + upper_adj + lax.psum(wpart, 'tok')]
    pallas_call x0 -> x1, Pallas kernels: none -> 170 us  [on_device(): pl.pallas_call(functools.partial(kernel, n, nv, scale), out_shape=(tok_sh...]
    dot_general x54 -> x0, matrix products: 36.2 us -> none  [matmul(): jnp.dot(left, right, precision=HIGH, preferred_element_type=jnp.float32)]
    reduce_sum x6 -> x0, other arithmetic: 5.87 us -> none  [the longest x2 3.16 us: colnorm(): return raised * (old / new)[..., None, :]]
  transfers between devices with their start and end apart: 4 -> 0, of which waited for: 4 -> 0; matrix products, arithmetic and copies ran while one was open for 7% -> 0% of each run, Pallas kernels for 0% -> 0%
where the time goes in v1:
time: 179 us
  Pallas kernels  170 us (95%)
  local copies, waits for them, and re-layouts  8.74 us (5%)
    pallas_call x1, Pallas kernels, on_device(): pl.pallas_call(functools.partial(kernel, n, nv, scale), out_shape=(tok_sh...  170 us
    unnamed x16, local copies, waits for them, and re-layouts  8.74 us

profile of v1, /device:TPU:6, one launch (start us, length us, event | category | flops | bytes accessed | tf_op | source)
XLA Modules:
  0.0 179.1 jit_solution(3847727164552625430)
XLA Ops:
  0.6 0.0 copy-start
  0.6 1.1 copy-done
  1.8 0.0 copy-start.1
  1.8 1.0 copy-done.1
  2.8 0.0 copy-start.2
  2.8 0.9 copy-done.2
  3.7 0.0 copy-start.3
  3.7 0.9 copy-done.3
  4.6 0.0 copy-start.4
  4.6 0.9 copy-done.4
  5.5 0.0 copy-start.5
  5.5 0.9 copy-done.5
  6.5 169.7 %shard_map.93 = (bf16[3,128,256]{2,1,0:T(8,128)(2,1)S(1)}, bf16[3,128,256]{2,1,0:T(8,128)(2,1)S(1)}, bf16[3,128,256]{2,1,0:T(8,128)(2,1)S(1)}, f32[3,256,256]{2,1,0:T(8,128)S(1)}) custom-call(bf16[3,128,256]{2,1,0:T(8,128)(2,1)S(1)} %bitcast.22, bf16[3,128,256]{2,1,0:T(8,128)(2,1)S(1)} %bitcast.23, bf16[3,128,256]{2,1,0:T(8,128)(2,1)S(1)} %bitcast.24, ...), custom_call_target="tpu_custom_call" | custom-call | tf_op jit(solution)/shard_map/pallas_call | solution.py:388
  176.2 0.7 copy.17
  176.8 0.7 copy.18
  177.5 0.7 copy.19
  178.2 0.9 copy.20
Async XLA Ops:
  0.6 1.1 copy-start
  1.8 1.0 copy-start.1
  2.8 0.9 copy-start.2
  3.7 0.9 copy-start.3
  4.6 0.9 copy-start.4
  5.5 0.9 copy-start.5

commit v2 on v1

v2 whole, which is shorter than its diff:
```python
import functools

import jax
import jax.numpy as jnp
from jax import lax
from jax.experimental import pallas as pl
from jax.experimental.pallas import tpu as pltpu
from jax.sharding import PartitionSpec as P

EPS = 1e-06
F32 = jnp.float32
BF16 = jnp.bfloat16
TREE = {1: 0, 3: 0, 2: 1, 4: 3, 6: 3, 5: 4, 7: 6, 8: 6}
FIXED, HOP = 2.2, 0.9
STAGGER = 1.0


def tree(n):
    half = n // 2
    if half == 8:
        up = dict(TREE)
    else:
        up = {d: d - 1 for d in range(1, half + 1)}
    parent = dict(up)
    for d, to in up.items():
        if d < n - half:
            parent[-d] = -to
    return parent


def depth(parent):
    t = {0: 0.0}
    for d in sorted(parent, key=lambda d: (abs(d), d)):
        chain = [d]
        while chain[-1] not in t:
            chain.append(parent[chain[-1]])
        for a, b in zip(chain[-2::-1], chain[:0:-1]):
            t[a] = t[b] + FIXED + HOP * abs(a - b)
    return t


def nn(a, b):
    return lax.dot_general(a, b, (((1,), (0,)), ((), ())), preferred_element_type=F32)


def nt(a, b):
    return lax.dot_general(a, b, (((1,), (1,)), ((), ())), preferred_element_type=F32)


def split(x):
    hi = x.astype(BF16)
    return hi, (x - hi.astype(F32)).astype(BF16)


def kernel(
    n, nv, scale, parent,
    q_h, k_h, v_h, o_h, init_h, upd_h,
    dq_r, dk_r, dv_r, ig_r,
    qv, kv, vv, ov, iv, uv,
    wb, ub, ut, mb, sv, pu, act, tt, rb, vb,
    in_sem, rs_ss, rs_rs, ag_ss, ag_rs, v_ss, v_rs,
):
    hd = iv.shape[1]
    sr = hd // n
    index = {d: i for i, d in enumerate(parent)}
    kids = {d: sorted((e for e in parent if parent[e] == d), key=lambda e: -abs(e)) for d in [0] + list(parent)}
    when = depth(parent)
    span = max(when.values())

    me = lax.axis_index("tok")
    core = lax.rem(lax.axis_index("head"), 2)
    vid = lax.axis_index("vid")
    flip = lambda i: lax.rem(i * (1 - core) + (n - i) * core, n)
    p = flip(me)
    jumps = sorted({(d - parent[d]) % n for d in parent} | {(parent[d] - d) % n for d in parent})
    device = {j: flip(lax.rem(p + j, n)) for j in jumps}

    barrier = pltpu.get_barrier_semaphore()
    for j in jumps:
        pl.semaphore_signal(barrier, inc=1, device_id={"tok": device[j]}, device_id_type=pl.DeviceIdType.MESH)
    for d in range(1, nv):
        pl.semaphore_signal(
            barrier, inc=1, device_id={"vid": lax.rem(vid + d, nv)}, device_id_type=pl.DeviceIdType.MESH
        )

    loads = {}

    def load(name, src, dst, i):
        loads[name] = pltpu.make_async_copy(src, dst, in_sem.at[i])
        loads[name].start()

    load("init", init_h, iv, 0)
    load("upd0", upd_h.at[0], uv.at[0], 1)
    load("upd1", upd_h.at[1], uv.at[1], 2)
    load("q2", q_h.at[2], qv.at[2], 3)
    load("o2", o_h.at[2], ov.at[2], 4)
    load("k1", k_h.at[1], kv.at[1], 5)
    load("v1", v_h.at[1], vv.at[1], 6)
    load("q1", q_h.at[1], qv.at[1], 7)
    load("o1", o_h.at[1], ov.at[1], 8)
    load("k0", k_h.at[0], kv.at[0], 9)
    load("v0", v_h.at[0], vv.at[0], 10)
    load("q0", q_h.at[0], qv.at[0], 11)
    load("o0", o_h.at[0], ov.at[0], 12)

    def rows(shard):
        return pl.ds(pl.multiple_of(lax.rem(shard + 2 * n, n) * sr, 8), sr)

    def weights(m):
        w = iv[m].astype(F32)
        for c in range(3):
            hi, lo = split(w)
            wb[c, m, 0] = hi
            wb[c, m, 1] = lo
            if c < 2:
                up = w + uv[c, m].astype(F32)
                old = jnp.sqrt(jnp.sum(w * w, axis=0, keepdims=True) + EPS)
                new = jnp.sqrt(jnp.sum(up * up, axis=0, keepdims=True) + EPS)
                w = up * (old / new)

    def xw(x, c, m):
        return nn(x, wb[c, m, 0]) + nn(x, wb[c, m, 1])

    def xwt(x, c, m):
        return nt(x, wb[c, m, 0]) + nt(x, wb[c, m, 1])

    def ywt(y, c, m):
        hi, lo = split(y)
        return nt(hi, wb[c, m, 0]) + nt(hi, wb[c, m, 1]) + nt(lo, wb[c, m, 0])

    def yw(y, c, m):
        hi, lo = split(y)
        return nn(hi, wb[c, m, 0]) + nn(hi, wb[c, m, 1]) + nn(lo, wb[c, m, 0])

    def left2(y, x):
        hi, lo = split(y)
        return nn(hi, x) + nn(lo, x)

    def right2(x, y):
        hi, lo = split(y)
        return nn(x, hi) + nn(x, lo)

    def t16(x):
        return x.astype(F32).T.astype(BF16)

    def query_a(c):
        loads[f"q{c}"].wait()
        g = xw(qv[c], c, 0)
        u = xw(qv[c], c, 1)
        s = jax.nn.sigmoid(g)
        a = g * s
        act[0] = u * (s * (1.0 + g * (1.0 - s)))
        act[1] = a
        act[2] = a * u

    def query_d(c):
        dh = xwt(ov[c], c, 2)
        act[0] = dh * act[0]
        act[1] = dh * act[1]

    def query_sum(c, m):
        if m == 2:
            loads[f"o{c}"].wait()
            mb[c, 2] = right2(t16(ov[c]), act[2]) if c else left2(act[2].T, ov[c])
        else:
            mb[c, m] = left2(act[m].T, qv[c]) if c else right2(t16(qv[c]), act[m])

    def query_c(c):
        dq_r[c] = (ywt(act[0], c, 0) + ywt(act[1], c, 1)).astype(BF16)

    def update_a(c):
        loads[f"k{c}"].wait()
        loads[f"v{c}"].wait()
        g = xw(kv[c], c, 0)
        u = xw(kv[c], c, 1)
        b = xwt(vv[c], c, 2)
        s = jax.nn.sigmoid(g)
        a = g * s * scale
        d1 = (s * (1.0 + g * (1.0 - s))) * scale
        d2 = (s * (1.0 - s) * (2.0 + g * (1.0 - 2.0 * s))) * scale
        act[3] = b * u * d2
        act[4] = b * d1
        act[5] = u * d1
        act[6] = a
        act[7] = b * u * d1
        act[8] = b * a
        act[9] = a * u

    def update_t(c):
        if c > 0:
            tt[...] = t16(vv[c])
        else:
            tt[...] = t16(kv[c])

    def kut(c, m):
        return nt(kv[c], ub[m, 0]) + nt(kv[c], ub[m, 1])

    def halves(c, m):
        hi, lo = split(ut[c, m])
        ub[m, 0] = hi
        ub[m, 1] = lo

    def after_gate(c):
        halves(c, 0)
        act[10] = kut(c, 0)

    def after_up(c):
        halves(c, 1)
        act[11] = kut(c, 1)

    def after_down(c):
        halves(c, 2)
        act[12] = nn(vv[c], ub[2, 0]) + nn(vv[c], ub[2, 1])

    def sum_gate(c):
        y = act[10] * act[3] + act[11] * act[4] + act[12] * act[5]
        act[0] = y
        mb[c, 0] += left2(y.T, kv[c]) if c else right2(tt[...], y)

    def sum_up(c):
        y = act[10] * act[4] + act[12] * act[6]
        act[1] = y
        mb[c, 1] += left2(y.T, kv[c]) if c else right2(tt[...], y)

    def sum_down(c):
        y = act[10] * act[5] + act[11] * act[6]
        act[2] = y
        mb[c, 2] += right2(tt[...], y) if c else left2(y.T, vv[c])

    def dot3(y, m, transposed):
        hi, lo = split(y)
        f = nt if transposed else nn
        return f(hi, ub[m, 0]) + f(hi, ub[m, 1]) + f(lo, ub[m, 0])

    def grads_a(c):
        dk_r[c] = (
            dot3(act[7], 0, False) + dot3(act[8], 1, False) + ywt(act[0], c, 0) + ywt(act[1], c, 1)
        ).astype(BF16)

    def grads_b(c):
        dv_r[c] = (dot3(act[9], 2, True) + yw(act[2], c, 2)).astype(BF16)

    def shard_rows():
        at = lax.broadcasted_iota(jnp.int32, (sr, hd), 1) - lax.broadcasted_iota(jnp.int32, (sr, hd), 0)
        pick = jnp.where(at == p * sr, 1.0, 0.0).astype(BF16)
        for m in range(3):
            w = nt(pick, iv[m])
            for c in range(2):
                up = w + nt(pick, uv[c, m])
                old = jnp.sqrt(jnp.sum(w * w, axis=1, keepdims=True) + EPS)
                new = jnp.sqrt(jnp.sum(up * up, axis=1, keepdims=True) + EPS)
                ratio = old / new
                sv[c, 0, m] = up
                sv[c, 1, m] = jnp.broadcast_to(ratio, up.shape)
                sv[c, 2, m] = up * (ratio / (new * new))
                sv[c, 3, m] = w / (old * new)
                w = up * ratio

    def place():
        at = lax.broadcasted_iota(jnp.int32, (sr, hd), 1) - lax.broadcasted_iota(jnp.int32, (sr, hd), 0)
        pick = jnp.where(at == p * sr, 1.0, 0.0)
        for m in range(3):
            mb[0, m] += lax.dot_general(
                pu[m], pick, (((0,), (0,)), ((), ())),
                precision=lax.Precision.HIGHEST, preferred_element_type=F32,
            )

    def copy_to(axis, index, src, dst, ss, rs):
        return pltpu.make_async_remote_copy(
            src_ref=src, dst_ref=dst, send_sem=ss, recv_sem=rs,
            device_id={axis: index}, device_id_type=pl.DeviceIdType.MESH,
        )

    sent = []

    def arrived(at, sem):
        copy_to("tok", device[jumps[0]], at, at, sem, sem).wait_recv()

    def collect(c, m, d):
        own = mb.at[c, m, rows(p - d)]
        if not kids[d]:
            return own
        total = None
        for e in kids[d]:
            at = rb.at[c, index[e], m]
            arrived(at, rs_rs.at[c, index[e], m])
            total = (own[...] if total is None else total) + at[...]
        if d == 0:
            return total
        at = rb.at[c, index[kids[d][0]], m]
        at[...] = total
        return at

    def reduce_send(c, m, d):
        i = index[d]
        cp = copy_to(
            "tok", device[(parent[d] - d) % n], collect(c, m, d), rb.at[c, i, m], rs_ss.at[c, i, m], rs_rs.at[c, i, m]
        )
        cp.start()
        sent.append(cp)

    def gather_send(c, buf, m, d):
        at = buf.at[m, rows(p - d)]
        for e in kids[d]:
            cp = copy_to(
                "tok", device[(e - d) % n], at, at, ag_ss.at[c, index[e], m], ag_rs.at[c, index[e], m]
            )
            cp.start()
            sent.append(cp)

    def gather_step(c, buf, m, d):
        arrived(buf.at[m, rows(p - d)], ag_rs.at[c, index[d], m])
        gather_send(c, buf, m, d)

    def norm_back(c, m, first):
        total = collect(c + 1, m, 0)
        if not first:
            total = total + pu[m]
        inner = jnp.sum(total * sv[c, 0, m], axis=1, keepdims=True)
        step = total * sv[c, 1, m] - inner * sv[c, 2, m]
        ut[c, m, rows(p)] = step
        gather_send(c + 1, ut.at[c], m, 0)
        pu[m] = step + inner * sv[c, 3, m]

    def to_videos(m):
        at = vb.at[vid, m]
        at[...] = collect(0, m, 0)
        for d in range(1, nv):
            cp = copy_to("vid", lax.rem(vid + d, nv), at, at, v_ss.at[d, m], v_rs.at[d, m])
            cp.start()
            sent.append(cp)

    def from_videos(m):
        for d in range(1, nv):
            arrived(vb.at[lax.rem(vid + nv - d, nv), m], v_rs.at[d, m])
        total = vb[0, m]
        for w in range(1, nv):
            total = total + vb[w, m]
        ig_r[m, rows(p)] = total
        gather_send(0, ig_r, m, 0)

    events = []
    queue = []

    def at(t, f, *args):
        events.append((t, len(events), functools.partial(f, *args)))

    def later(*fs):
        queue.extend(fs)

    def flush():
        while queue:
            queue.pop(0)()

    def exchange(c, starts, finish, extra, buf):
        ends = {}
        for m, t in starts.items():
            for d in parent:
                at(t + span - when[d], reduce_send, c, m, d)
            t += span + 0.2
            at(t, finish, m)
            if extra:
                t += extra
                at(t, from_videos, m)
            for d in parent:
                at(t + 0.2 + when[d], gather_step, c, buf, m, d)
            ends[m] = t + 0.2 + span
        return ends

    done = set()

    def once(f, *args):
        if (f, args) not in done:
            done.add((f, args))
            f(*args)

    def zeros():
        dk_r[2] = jnp.zeros(dk_r.shape[1:], BF16)
        dv_r[2] = jnp.zeros(dv_r.shape[1:], BF16)

    for name in ("init", "upd0", "upd1"):
        loads[name].wait()
    weights(0)
    weights(1)
    query_a(2)
    query_sum(2, 2)
    pl.semaphore_wait(barrier, len(jumps) + nv - 1)

    def first_rest():
        weights(2)
        query_d(2)
        query_sum(2, 0)

    at(0.01, first_rest)
    at(STAGGER - 0.01, query_sum, 2, 1)
    later(
        functools.partial(once, shard_rows), lambda: query_c(2), lambda: update_a(1), lambda: update_t(1),
        lambda: query_a(1), lambda: query_sum(1, 2), lambda: query_d(1), lambda: query_sum(1, 0),
        lambda: query_sum(1, 1), lambda: query_c(1), zeros,
    )
    ends = exchange(
        2, {2: 0.0, 0: STAGGER, 1: 2 * STAGGER},
        lambda m: (once(shard_rows), norm_back(1, m, True)), 0, ut.at[1],
    )
    at(ends[2] + 0.01, lambda: (flush(), after_down(1)))
    at(ends[0] + 0.01, lambda: (after_gate(1), sum_up(1)))
    at(ends[1] + 0.01, lambda: (after_up(1), sum_down(1)))
    t1 = {1: ends[0] + 0.5, 2: ends[1] + 0.5, 0: ends[1] + 0.5 + STAGGER}
    at(t1[2] + 0.01, lambda: (sum_gate(1), later(
        lambda: grads_a(1), lambda: grads_b(1), lambda: update_a(0), lambda: update_t(0),
        lambda: query_a(0), lambda: query_sum(0, 2), lambda: query_d(0), lambda: query_sum(0, 0),
        lambda: query_sum(0, 1), lambda: query_c(0),
    )))
    ends = exchange(1, t1, lambda m: norm_back(0, m, False), 0, ut.at[0])
    at(max(t1.values()) + span + 0.3, later, place)
    at(ends[1] + 0.01, lambda: (flush(), after_up(0)))
    at(ends[2] + 0.01, after_down, 0)
    at(ends[0] + 0.01, lambda: (after_gate(0), sum_up(0)))
    t0 = {1: ends[0] + 0.5, 2: ends[0] + 0.5 + STAGGER, 0: ends[0] + 0.5 + 2 * STAGGER}
    at(t0[1] + 0.01, sum_down, 0)
    at(t0[2] + 0.01, lambda: (sum_gate(0), later(lambda: grads_a(0), lambda: grads_b(0))))
    exchange(0, t0, to_videos, FIXED + 2 * HOP, ig_r)

    events.sort(key=lambda e: e[:2])
    for (t, _, f), after in zip(events, events[1:] + [(events[-1][0] + 9.0,)]):
        f()
        gap = after[0] - t
        while queue and gap > 0.45:
            queue.pop(0)()
            gap -= 0.7
    flush()
    for cp in sent:
        cp.wait_send()


def on_device(n, nv, queries, keys, values, out_grad, fast_init, updates):
    _, groups, tokens, _, hd = queries.shape
    scale = float(tokens * n) ** (-0.5)
    sr = hd // n
    parent = tree(n)
    edges = len(parent)
    flat = lambda x: x.reshape(groups, tokens, hd)
    hbm = pl.BlockSpec(memory_space=pltpu.HBM)
    vspec = pl.BlockSpec(memory_space=pltpu.VMEM)
    dma = pltpu.SemaphoreType.DMA
    tok_shape = jax.ShapeDtypeStruct((groups, tokens, hd), BF16)
    dq, dk, dv, ig = pl.pallas_call(
        functools.partial(kernel, n, nv, scale, parent),
        out_shape=(tok_shape, tok_shape, tok_shape, jax.ShapeDtypeStruct((3, hd, hd), F32)),
        in_specs=[hbm] * 6,
        out_specs=[vspec] * 4,
        scratch_shapes=[
            pltpu.VMEM((groups, tokens, hd), BF16),
            pltpu.VMEM((groups, tokens, hd), BF16),
            pltpu.VMEM((groups, tokens, hd), BF16),
            pltpu.VMEM((groups, tokens, hd), BF16),
            pltpu.VMEM((3, hd, hd), BF16),
            pltpu.VMEM((2, 3, hd, hd), BF16),
            pltpu.VMEM((3, 3, 2, hd, hd), BF16),
            pltpu.VMEM((3, 2, hd, hd), BF16),
            pltpu.VMEM((2, 3, hd, hd), F32),
            pltpu.VMEM((3, 3, hd, hd), F32),
            pltpu.VMEM((2, 4, 3, sr, hd), F32),
            pltpu.VMEM((3, sr, hd), F32),
            pltpu.VMEM((13, tokens, hd), F32),
            pltpu.VMEM((hd, tokens), BF16),
            pltpu.VMEM((3, edges, 3, sr, hd), F32),
            pltpu.VMEM((nv, 3, sr, hd), F32),
            dma((13,)),
            dma((3, edges, 3)), dma((3, edges, 3)),
            dma((3, edges, 3)), dma((3, edges, 3)),
            dma((nv, 3)), dma((nv, 3)),
        ],
        compiler_params=pltpu.CompilerParams(
            collective_id=0, has_side_effects=True, vmem_limit_bytes=48 * 1024 * 1024
        ),
    )(
        flat(queries), flat(keys), flat(values), flat(out_grad),
        fast_init.reshape(3, hd, hd), updates.reshape(groups - 1, 3, hd, hd),
    )
    shaped = lambda x: x.reshape(queries.shape)
    return shaped(dq), shaped(dk), shaped(dv), ig.reshape(fast_init.shape)


def solution(mesh):
    return jax.shard_map(
        functools.partial(on_device, mesh.shape["tok"], mesh.shape["vid"]),
        mesh=mesh,
        in_specs=(
            P("vid", None, "tok", "head", None),
            P("vid", None, "tok", "head", None),
            P("vid", None, "tok", "head", None),
            P("vid", None, "tok", "head", None),
            P("head", None, None, None),
            P("vid", None, "head", None, None, None),
        ),
        out_specs=(
            P("vid", None, "tok", "head", None),
            P("vid", None, "tok", "head", None),
            P("vid", None, "tok", "head", None),
            P("head", None, None, None),
        ),
        check_vma=False,
    )
```

time: 179 us -> 130 us (0.73)
  Pallas kernels: 170 us -> 120 us
    pallas_call x1, Pallas kernels: 170 us -> 120 us  [on_device(): pl.pallas_call(functools.partial(kernel, n, nv, scale, parent), out_shape...]
where the time goes in v2:
time: 130 us
  Pallas kernels  120 us (92%)
  local copies, waits for them, and re-layouts  8.74 us (7%)
    pallas_call x1, Pallas kernels, on_device(): pl.pallas_call(functools.partial(kernel, n, nv, scale, parent), out_shape...  120 us
    unnamed x16, local copies, waits for them, and re-layouts  8.74 us

profile of v2, /device:TPU:6, one launch (start us, length us, event | category | flops | bytes accessed | tf_op | source)
XLA Modules:
  0.0 129.9 jit_solution(5096067948972452827)
XLA Ops:
  0.6 0.0 copy-start
  0.6 1.1 copy-done
  1.8 0.0 copy-start.1
  1.8 1.0 copy-done.1
  2.8 0.0 copy-start.2
  2.8 0.9 copy-done.2
  3.7 0.0 copy-start.3
  3.7 0.9 copy-done.3
  4.6 0.0 copy-start.4
  4.6 0.9 copy-done.4
  5.5 0.0 copy-start.5
  5.5 0.9 copy-done.5
  6.5 120.5 %shard_map.93 = (bf16[3,128,256]{2,1,0:T(8,128)(2,1)S(1)}, bf16[3,128,256]{2,1,0:T(8,128)(2,1)S(1)}, bf16[3,128,256]{2,1,0:T(8,128)(2,1)S(1)}, f32[3,256,256]{2,1,0:T(8,128)S(1)}) custom-call(bf16[3,128,256]{2,1,0:T(8,128)(2,1)S(1)} %bitcast.22, bf16[3,128,256]{2,1,0:T(8,128)(2,1)S(1)} %bitcast.23, bf16[3,128,256]{2,1,0:T(8,128)(2,1)S(1)} %bitcast.24, ...), custom_call_target="tpu_custom_call" | custom-call | tf_op jit(solution)/shard_map/pallas_call | solution.py:447
  127.0 0.7 copy.17
  127.6 0.7 copy.18
  128.3 0.7 copy.19
  129.0 0.9 copy.20
Async XLA Ops:
  0.6 1.1 copy-start
  1.8 1.0 copy-start.1
  2.8 0.9 copy-start.2
  3.7 0.9 copy-start.3
  4.6 0.9 copy-start.4
  5.5 0.9 copy-start.5

commit v3 on v2

--- a/solution.py
+++ b/solution.py
@@ -11,8 +11,8 @@
 F32 = jnp.float32
 BF16 = jnp.bfloat16
 TREE = {1: 0, 3: 0, 2: 1, 4: 3, 6: 3, 5: 4, 7: 6, 8: 6}
-FIXED, HOP = 2.2, 0.9
-STAGGER = 1.0
+FIXED, HOP = 4.5, 0.4
+STAGGER = 1.5
 
 
 def tree(n):
@@ -431,6 +431,15 @@
     flush()
     for cp in sent:
         cp.wait_send()
+
+
+def store(n, *refs):
+    sem = refs[-1]
+    copies = [pltpu.make_async_copy(refs[i], refs[n + i], sem.at[i]) for i in range(n)]
+    for cp in copies:
+        cp.start()
+    for cp in copies:
+        cp.wait()
 
 
 def on_device(n, nv, queries, keys, values, out_grad, fast_init, updates):
@@ -475,9 +484,23 @@
             collective_id=0, has_side_effects=True, vmem_limit_bytes=48 * 1024 * 1024
         ),
     )(
-        flat(queries), flat(keys), flat(values), flat(out_grad),
-        fast_init.reshape(3, hd, hd), updates.reshape(groups - 1, 3, hd, hd),
+        *(
+            pltpu.with_memory_space_constraint(x, pltpu.HBM)
+            for x in (
+                flat(queries), flat(keys), flat(values), flat(out_grad),
+                fast_init.reshape(3, hd, hd), updates.reshape(groups - 1, 3, hd, hd),
+            )
+        ),
     )
+    outs = (dq, dk, dv, ig)
+    dq, dk, dv, ig = pl.pallas_call(
+        functools.partial(store, len(outs)),
+        out_shape=tuple(jax.ShapeDtypeStruct(x.shape, x.dtype) for x in outs),
+        in_specs=[vspec] * len(outs),
+        out_specs=[hbm] * len(outs),
+        scratch_shapes=[dma((len(outs),))],
+        compiler_params=pltpu.CompilerParams(vmem_limit_bytes=4 * 1024 * 1024),
+    )(*outs)
     shaped = lambda x: x.reshape(queries.shape)
     return shaped(dq), shaped(dk), shaped(dv), ig.reshape(fast_init.shape)
 

time: 130 us -> 115 us (0.88)
  local copies, waits for them, and re-layouts: 8.74 us -> 0 us
  Pallas kernels: 120 us -> 114 us
    unnamed x16 -> x0, local copies, waits for them, and re-layouts: 8.74 us -> none
    pallas_call x1, Pallas kernels: 120 us -> 113 us  [on_device(): pl.pallas_call(functools.partial(kernel, n, nv, scale, parent), out_shape...]
where the time goes in v3:
time: 115 us
  Pallas kernels  114 us (99%)
    pallas_call x1, Pallas kernels, on_device(): pl.pallas_call(functools.partial(kernel, n, nv, scale, parent), out_shape...  113 us

profile of v3, /device:TPU:6, one launch (start us, length us, event | category | flops | bytes accessed | tf_op | source)
XLA Modules:
  0.0 114.5 jit_solution(3579755360372619266)
XLA Ops:
  0.6 112.8 %shard_map.93 = (bf16[3,128,256]{2,1,0:T(8,128)(2,1)S(1)}, bf16[3,128,256]{2,1,0:T(8,128)(2,1)S(1)}, bf16[3,128,256]{2,1,0:T(8,128)(2,1)S(1)}, f32[3,256,256]{2,1,0:T(8,128)S(1)}) custom-call(bf16[3,128,256]{2,1,0:T(8,128)(2,1)} %bitcast.18, bf16[3,128,256]{2,1,0:T(8,128)(2,1)} %bitcast.19, bf16[3,128,256]{2,1,0:T(8,128)(2,1)} %bitcast.20, ...), custom_call_target="tpu_custom_call" | custom-call | tf_op jit(solution)/shard_map/pallas_call | solution.py:456
  113.4 1.1 shard_map.94

commit v4 on v3

--- a/solution.py
+++ b/solution.py
@@ -10,15 +10,18 @@
 EPS = 1e-06
 F32 = jnp.float32
 BF16 = jnp.bfloat16
-TREE = {1: 0, 3: 0, 2: 1, 4: 3, 6: 3, 5: 4, 7: 6, 8: 6}
+TREES = (
+    {1: 0, 3: 0, 2: 1, 4: 3, 6: 3, 5: 4, 7: 6, 8: 6},
+    {1: 0, 2: 0, 3: 2, 4: 2, 5: 4, 6: 4, 7: 6, 8: 6},
+)
 FIXED, HOP = 4.5, 0.4
 STAGGER = 1.5
 
 
-def tree(n):
+def tree(n, core):
     half = n // 2
     if half == 8:
-        up = dict(TREE)
+        up = dict(TREES[core])
     else:
         up = {d: d - 1 for d in range(1, half + 1)}
     parent = dict(up)
@@ -52,8 +55,14 @@
     return hi, (x - hi.astype(F32)).astype(BF16)
 
 
-def kernel(
-    n, nv, scale, parent,
+def kernel(n, nv, scale, *refs):
+    which = lax.rem(lax.axis_index("head"), 2)
+    for core in range(2):
+        pl.when(which == core)(functools.partial(body, n, nv, scale, core, *refs))
+
+
+def body(
+    n, nv, scale, core,
     q_h, k_h, v_h, o_h, init_h, upd_h,
     dq_r, dk_r, dv_r, ig_r,
     qv, kv, vv, ov, iv, uv,
@@ -62,15 +71,15 @@
 ):
     hd = iv.shape[1]
     sr = hd // n
+    parent = tree(n, core)
     index = {d: i for i, d in enumerate(parent)}
     kids = {d: sorted((e for e in parent if parent[e] == d), key=lambda e: -abs(e)) for d in [0] + list(parent)}
     when = depth(parent)
     span = max(when.values())
 
     me = lax.axis_index("tok")
-    core = lax.rem(lax.axis_index("head"), 2)
     vid = lax.axis_index("vid")
-    flip = lambda i: lax.rem(i * (1 - core) + (n - i) * core, n)
+    flip = lambda i: lax.rem(n - i, n) if core else i
     p = flip(me)
     jumps = sorted({(d - parent[d]) % n for d in parent} | {(parent[d] - d) % n for d in parent})
     device = {j: flip(lax.rem(p + j, n)) for j in jumps}
@@ -404,9 +413,9 @@
     )
     at(ends[2] + 0.01, lambda: (flush(), after_down(1)))
     at(ends[0] + 0.01, lambda: (after_gate(1), sum_up(1)))
-    at(ends[1] + 0.01, lambda: (after_up(1), sum_down(1)))
-    t1 = {1: ends[0] + 0.5, 2: ends[1] + 0.5, 0: ends[1] + 0.5 + STAGGER}
-    at(t1[2] + 0.01, lambda: (sum_gate(1), later(
+    at(ends[1] + 0.01, lambda: (after_up(1), sum_gate(1)))
+    t1 = {1: ends[0] + 0.5, 0: ends[1] + 0.5, 2: ends[1] + 0.5 + STAGGER}
+    at(t1[0] + 0.01, lambda: (sum_down(1), later(
         lambda: grads_a(1), lambda: grads_b(1), lambda: update_a(0), lambda: update_t(0),
         lambda: query_a(0), lambda: query_sum(0, 2), lambda: query_d(0), lambda: query_sum(0, 0),
         lambda: query_sum(0, 1), lambda: query_c(0),
@@ -414,11 +423,10 @@
     ends = exchange(1, t1, lambda m: norm_back(0, m, False), 0, ut.at[0])
     at(max(t1.values()) + span + 0.3, later, place)
     at(ends[1] + 0.01, lambda: (flush(), after_up(0)))
-    at(ends[2] + 0.01, after_down, 0)
-    at(ends[0] + 0.01, lambda: (after_gate(0), sum_up(0)))
-    t0 = {1: ends[0] + 0.5, 2: ends[0] + 0.5 + STAGGER, 0: ends[0] + 0.5 + 2 * STAGGER}
-    at(t0[1] + 0.01, sum_down, 0)
-    at(t0[2] + 0.01, lambda: (sum_gate(0), later(lambda: grads_a(0), lambda: grads_b(0))))
+    at(ends[0] + 0.01, lambda: (after_gate(0), sum_down(0)))
+    at(ends[2] + 0.01, lambda: (after_down(0), sum_up(0)))
+    t0 = {2: ends[0] + 0.5, 1: ends[2] + 0.5, 0: ends[2] + 0.5 + STAGGER}
+    at(t0[1] + 0.01, lambda: (sum_gate(0), later(lambda: grads_a(0), lambda: grads_b(0))))
     exchange(0, t0, to_videos, FIXED + 2 * HOP, ig_r)
 
     events.sort(key=lambda e: e[:2])
@@ -446,15 +454,14 @@
     _, groups, tokens, _, hd = queries.shape
     scale = float(tokens * n) ** (-0.5)
     sr = hd // n
-    parent = tree(n)
-    edges = len(parent)
+    edges = n - 1
     flat = lambda x: x.reshape(groups, tokens, hd)
     hbm = pl.BlockSpec(memory_space=pltpu.HBM)
     vspec = pl.BlockSpec(memory_space=pltpu.VMEM)
     dma = pltpu.SemaphoreType.DMA
     tok_shape = jax.ShapeDtypeStruct((groups, tokens, hd), BF16)
     dq, dk, dv, ig = pl.pallas_call(
-        functools.partial(kernel, n, nv, scale, parent),
+        functools.partial(kernel, n, nv, scale),
         out_shape=(tok_shape, tok_shape, tok_shape, jax.ShapeDtypeStruct((3, hd, hd), F32)),
         in_specs=[hbm] * 6,
         out_specs=[vspec] * 4,

time: 115 us -> 112 us (0.974)
  Pallas kernels: 114 us -> 110 us
    pallas_call x1, Pallas kernels: 113 us -> 109 us  [on_device(): pl.pallas_call(functools.partial(kernel, n, nv, scale), out_shape=(tok_sh...]
where the time goes in v4:
time: 112 us; the launch traced here: 111 us
  Pallas kernels  110 us (98%)
    pallas_call x1, Pallas kernels, on_device(): pl.pallas_call(functools.partial(kernel, n, nv, scale), out_shape=(tok_sh...  109 us

profile of v4, /device:TPU:6, one launch (start us, length us, event | category | flops | bytes accessed | tf_op | source)
XLA Modules:
  0.0 111.3 jit_solution(614707375655214683)
XLA Ops:
  0.6 109.4 %shard_map.93 = (bf16[3,128,256]{2,1,0:T(8,128)(2,1)S(1)}, bf16[3,128,256]{2,1,0:T(8,128)(2,1)S(1)}, bf16[3,128,256]{2,1,0:T(8,128)(2,1)S(1)}, f32[3,256,256]{2,1,0:T(8,128)S(1)}) custom-call(bf16[3,128,256]{2,1,0:T(8,128)(2,1)} %bitcast.18, bf16[3,128,256]{2,1,0:T(8,128)(2,1)} %bitcast.19, bf16[3,128,256]{2,1,0:T(8,128)(2,1)} %bitcast.20, ...), custom_call_target="tpu_custom_call" | custom-call | tf_op jit(solution)/shard_map/pallas_call | solution.py:463
  110.0 1.1 shard_map.94

commit v5 on v4

--- a/solution.py
+++ b/solution.py
@@ -115,13 +115,14 @@
     def rows(shard):
         return pl.ds(pl.multiple_of(lax.rem(shard + 2 * n, n) * sr, 8), sr)
 
-    def weights(m):
+    def weights(m, groups):
         w = iv[m].astype(F32)
-        for c in range(3):
-            hi, lo = split(w)
-            wb[c, m, 0] = hi
-            wb[c, m, 1] = lo
-            if c < 2:
+        for c in range(max(groups) + 1):
+            if c in groups:
+                hi, lo = split(w)
+                wb[c, m, 0] = hi
+                wb[c, m, 1] = lo
+            if c < max(groups):
                 up = w + uv[c, m].astype(F32)
                 old = jnp.sqrt(jnp.sum(w * w, axis=0, keepdims=True) + EPS)
                 new = jnp.sqrt(jnp.sum(up * up, axis=0, keepdims=True) + EPS)
@@ -389,21 +390,22 @@
 
     for name in ("init", "upd0", "upd1"):
         loads[name].wait()
-    weights(0)
-    weights(1)
+    weights(0, (2,))
+    weights(1, (2,))
     query_a(2)
     query_sum(2, 2)
     pl.semaphore_wait(barrier, len(jumps) + nv - 1)
 
     def first_rest():
-        weights(2)
+        weights(2, (2,))
         query_d(2)
         query_sum(2, 0)
 
     at(0.01, first_rest)
     at(STAGGER - 0.01, query_sum, 2, 1)
     later(
-        functools.partial(once, shard_rows), lambda: query_c(2), lambda: update_a(1), lambda: update_t(1),
+        functools.partial(once, shard_rows), lambda: query_c(2), lambda: weights(0, (0, 1)), lambda: weights(1, (0, 1)),
+        lambda: weights(2, (0, 1)), lambda: update_a(1), lambda: update_t(1),
         lambda: query_a(1), lambda: query_sum(1, 2), lambda: query_d(1), lambda: query_sum(1, 0),
         lambda: query_sum(1, 1), lambda: query_c(1), zeros,
     )

time: 112 us -> 112 us (level)
  no operation moved by 1% of the time
where the time goes in v5:
time: 112 us; the launch traced here: 111 us
  Pallas kernels  111 us (99%)
    pallas_call x1, Pallas kernels, on_device(): pl.pallas_call(functools.partial(kernel, n, nv, scale), out_shape=(tok_sh...  110 us

profile of v5, /device:TPU:6, one launch (start us, length us, event | category | flops | bytes accessed | tf_op | source)
XLA Modules:
  0.0 111.4 jit_solution(344141022513055289)
XLA Ops:
  0.6 109.5 %shard_map.93 = (bf16[3,128,256]{2,1,0:T(8,128)(2,1)S(1)}, bf16[3,128,256]{2,1,0:T(8,128)(2,1)S(1)}, bf16[3,128,256]{2,1,0:T(8,128)(2,1)S(1)}, f32[3,256,256]{2,1,0:T(8,128)S(1)}) custom-call(bf16[3,128,256]{2,1,0:T(8,128)(2,1)} %bitcast.18, bf16[3,128,256]{2,1,0:T(8,128)(2,1)} %bitcast.19, bf16[3,128,256]{2,1,0:T(8,128)(2,1)} %bitcast.20, ...), custom_call_target="tpu_custom_call" | custom-call | tf_op jit(solution)/shard_map/pallas_call | solution.py:465
  110.2 1.1 shard_map.94
